TPU v7x, 512 devices: a whole 4x8x8 slice. The times are simulated.
512 devices in a mesh: dp: 64 (over z_lo, y, core), expert: 8 (over x, z_hi).
Axes of the slice: x: 4, y: 8, z: 8 (z_hi: 2, z_lo: 4; z = z_hi * 4 + z_lo), core: 2. Of those that a mesh axis runs over, the one named last changes fastest.
Arguments:
- tokens: bfloat16 [131072, 1024], P(('dp', 'expert')), may hold values from -6 to 6
- expert_ids: int32 [131072], P(('dp', 'expert')), may hold values from 0 to 7
- slots: int32 [131072], P(('dp', 'expert')), may hold values from -1 to 39, as said below
- router: bfloat16 [1024, 8], replicated, may hold values from -0.1875 to 0.1875
- w_in: bfloat16 [8, 1024, 2048], P('expert', 'dp'), may hold values from -0.1875 to 0.1875
- w_out: bfloat16 [8, 2048, 1024], P('expert', None, 'dp'), may hold values from -0.125 to 0.125
- texts: bfloat16 [2048, 1024], P(('dp', 'expert')), may hold values from -6 to 6
Outputs:
- d_tokens: bfloat16 [131072, 1024], P(('dp', 'expert'))
- d_texts: float32 [2048, 1024], P(('dp', 'expert'))
- router_grad: float32 [1024, 8], replicated
Inputs may be any that keep to these rules, and one draw needn't show every extreme that they name: Within each block of 256 tokens (one device's), the tokens of each expert hold slots 0, 1, 2, ... in token order until 40, and -1 after. On every index of dp, some expert receives all 40 slots from each of the 8 blocks of that index.
All inputs are finite; a program needn't handle non-finite values.
Results may differ from a plain program's by a relative error of at most 0.0064.
Values may be sent and summed in bfloat16 or wider, within the bound.
No kernel may reach another device: no remote copies, remote signals or barrier semaphores. Data moves between devices by JAX's collectives and lax.ppermute only.
A program may use at most 64 MiB of HBM per device.

v0:
```python
import jax
import jax.numpy as jnp
from jax import lax
from jax.sharding import PartitionSpec as P

highest = lax.Precision.HIGHEST
temper = 10.0
offset = -2.0
loss_scale = 256.0
epsilon = 1e-06


def shifted(block, axis, distance):
    devices = range(lax.axis_size(axis))
    route = [((i - distance) % len(devices), i) for i in devices]
    return lax.ppermute(block, axis, route)


def gelu_slope(hidden):
    result, pullback = jax.vjp(lambda inputs: jax.nn.gelu(inputs, approximate=True), hidden)
    return pullback(jnp.ones_like(hidden))[0]


def contract_last(left, right):
    return lax.dot_general(
        left, right, (((1,), (1,)), ((), ())), preferred_element_type=jnp.float32
    )


def unit_rows(matrix):
    values_float = matrix.astype(jnp.float32)
    scales = lax.rsqrt(jnp.sum(values_float * values_float, axis=1, keepdims=True) + epsilon)
    return (values_float * scales, scales)


def body(tokens, expert_ids, slots, router, w_in, w_out, texts):
    tok_count, model_width = tokens.shape
    experts = router.shape[1]
    capacity = 5 * tok_count // (4 * experts)
    images = texts.shape[0]
    patch_len = tok_count // images
    is_kept = slots >= 0
    kept_float = is_kept.astype(jnp.float32)
    columns = jnp.arange(experts, dtype=jnp.int32)
    chosen = (expert_ids[:, None] == columns[None, :]).astype(jnp.float32)
    logits = jnp.dot(tokens, router, preferred_element_type=jnp.float32)
    gate_values = jax.nn.sigmoid(jnp.sum(logits * chosen, axis=1))
    slot_total = experts * capacity
    places = jnp.where(is_kept, expert_ids * capacity + slots, slot_total)
    safe_places = jnp.minimum(places, slot_total - 1)
    send_buffer = (
        jnp.zeros((slot_total, model_width), jnp.bfloat16).at[places].set(tokens, mode="drop")
    )
    arrived = lax.all_to_all(
        send_buffer.reshape(experts, capacity, model_width),
        "expert",
        split_axis=0,
        concat_axis=0,
        tiled=True,
    )
    sources = arrived.shape[0]
    routed = arrived.reshape(sources * capacity, model_width)
    row_count = routed.shape[0]
    in_full, out_full = (
        lax.all_gather(w_in, "dp", axis=1, tiled=True),
        lax.all_gather(w_out, "dp", axis=2, tiled=True),
    )
    in_matrix = in_full[0]
    out_matrix = out_full[0]
    hidden = jnp.dot(routed, in_matrix, preferred_element_type=jnp.float32)
    active = jax.nn.gelu(hidden, approximate=True).astype(jnp.bfloat16)
    expert_out = jnp.dot(active, out_matrix, preferred_element_type=jnp.float32).astype(
        jnp.bfloat16
    )
    returned_rows = lax.all_to_all(
        expert_out.reshape(sources, capacity, model_width),
        "expert",
        split_axis=0,
        concat_axis=0,
        tiled=True,
    )
    combined = jnp.where(
        is_kept[:, None],
        returned_rows.reshape(slot_total, model_width)[safe_places].astype(jnp.float32),
        0.0,
    )
    branch = gate_values[:, None] * combined
    pooled = jnp.mean(branch.reshape(images, patch_len, model_width), axis=1)
    unit_img, pooled_scale = unit_rows(pooled)
    neighbour = shifted(texts, "dp", 1)
    own_unit, own_scale = unit_rows(texts)
    next_unit, unused = unit_rows(neighbour)
    diagonal = jnp.eye(images, dtype=jnp.float32)
    own_scores = temper * jnp.dot(unit_img, own_unit.T, precision=highest) + offset
    next_scores = temper * jnp.dot(unit_img, next_unit.T, precision=highest) + offset
    own_grad = loss_scale * (jax.nn.sigmoid(own_scores) - diagonal)
    next_grad = loss_scale * jax.nn.sigmoid(next_scores)
    grad_image = temper * (
        jnp.dot(own_grad, own_unit, precision=highest)
        + jnp.dot(next_grad, next_unit, precision=highest)
    )
    grad_text_own = temper * jnp.dot(own_grad.T, unit_img, precision=highest)
    grad_text_next = temper * jnp.dot(next_grad.T, unit_img, precision=highest)
    grad_text_back = shifted(grad_text_next, "dp", -1)
    grad_text = grad_text_own + grad_text_back
    d_texts = (
        grad_text - own_unit * jnp.sum(own_unit * grad_text, axis=1, keepdims=True)
    ) * own_scale
    grad_pooled = (
        grad_image - unit_img * jnp.sum(unit_img * grad_image, axis=1, keepdims=True)
    ) * pooled_scale
    grad_branch = jnp.broadcast_to(
        grad_pooled[:, None, :] / patch_len, (images, patch_len, model_width)
    ).reshape(tok_count, model_width)
    grad_combined = (gate_values[:, None] * grad_branch).astype(jnp.bfloat16)
    grad_buffer = (
        jnp.zeros((slot_total, model_width), jnp.bfloat16)
        .at[places]
        .set(grad_combined, mode="drop")
    )
    grad_gate = jnp.sum(grad_branch * combined, axis=1)
    grad_logits = chosen * (grad_gate * gate_values * (1.0 - gate_values) * kept_float)[:, None]
    partial_value = jnp.dot(tokens.astype(jnp.float32).T, grad_logits, precision=highest)
    router_grad = lax.psum(partial_value, ("dp", "expert"))
    router_part = jnp.dot(grad_logits, router.astype(jnp.float32).T, precision=highest)
    grads_in = lax.all_to_all(
        grad_buffer.reshape(experts, capacity, model_width),
        "expert",
        split_axis=0,
        concat_axis=0,
        tiled=True,
    )
    grads_in = grads_in.reshape(row_count, model_width)
    slopes = gelu_slope(hidden)
    grad_hidden = (contract_last(grads_in, out_matrix) * slopes).astype(jnp.bfloat16)
    grad_routed = contract_last(grad_hidden, in_matrix).astype(jnp.bfloat16)
    grad_back = lax.all_to_all(
        grad_routed.reshape(sources, capacity, model_width),
        "expert",
        split_axis=0,
        concat_axis=0,
        tiled=True,
    )
    grad_tokens = jnp.where(
        is_kept[:, None],
        grad_back.reshape(slot_total, model_width)[safe_places].astype(jnp.float32),
        0.0,
    )
    d_tokens = (grad_tokens + router_part).astype(jnp.bfloat16)
    return (d_tokens, d_texts, router_grad)


def solution(mesh):
    in_specs = (
        P(("dp", "expert"), None),
        P(("dp", "expert")),
        P(("dp", "expert")),
        P(),
        P("expert", "dp", None),
        P("expert", None, "dp"),
        P(("dp", "expert"), None),
    )
    out_specs = (P(("dp", "expert"), None), P(("dp", "expert"), None), P())
    return jax.shard_map(body, mesh=mesh, in_specs=in_specs, out_specs=out_specs, check_vma=False)
```

profile of v0, /device:TPU:1, one launch (start us, length us, event | category | flops | bytes accessed | tf_op | source)
XLA Modules:
  0.0 448.0 jit_solution(9497182288706210727)
XLA Ops:
  7.2 0.0 copy-start
  7.2 0.0 all-gather.3.cloned.1.call-start
  7.2 0.7 all-gather.3.cloned.1.call-update
  7.9 0.0 all-gather.5.cloned.1.call-start
  8.0 0.7 all-gather.5.cloned.1.call-update
  8.7 0.7 compare_select_fusion
  9.4 3.1 scatter_custom_fusion
  12.5 13.3 %all-to-all-start = ((bf16[8,40,1024]{2,1,0:T(8,128)(2,1)}), bf16[8,40,1024]{2,1,0:T(8,128)(2,1)S(1)}, u32[]{:S(2)}, u32[]{:S(2)}) async-start(bf16[8,40,1024]{2,1,0:T(8,128)(2,1)} %bitcast), calls=%async_computation | async-start | bytes 1310720 | tf_op jit(solution)/shard_map/all_to_all | solution.py:54
  25.7 4.0 collective-permute-start
  29.8 1.3 fusion.33
  31.1 10.3 %all-to-all-done = bf16[8,40,1024]{2,1,0:T(8,128)(2,1)S(1)} async-done(((bf16[8,40,1024]{2,1,0:T(8,128)(2,1)}), bf16[8,40,1024]{2,1,0:T(8,128)(2,1)S(1)}, u32[]{:S(2)}, u32[]{:S(2)}) %all-to-all-start) | async-done | bytes 655392 | tf_op jit(solution)/shard_map/all_to_all | solution.py:54
  41.4 98.3 %all-gather.3.cloned.1.call-done = bf16[1,1024,2048]{2,1,0:T(8,128)(2,1)} async-done(((bf16[1,16,2048]{2,1,0:T(8,128)(2,1)}), bf16[1,1024,2048]{2,1,0:T(8,128)(2,1)}) %all-gather.3.cloned.1.call-update) | async-done | bytes 4194320 | tf_op jit(solution)/shard_map/all_gather | solution.py:65
  139.6 3.7 fusion.6
  143.4 0.0 copy-start.2
  143.4 0.0 copy-start.4
  143.4 119.5 %all-gather.5.cloned.1.call-done = bf16[1,2048,1024]{1,2,0:T(8,128)(2,1)} async-done(((bf16[1,2048,16]{1,2,0:T(8,128)(2,1)}), bf16[1,2048,1024]{1,2,0:T(8,128)(2,1)}) %all-gather.5.cloned.1.call-update) | async-done | bytes 4194320 | tf_op jit(solution)/shard_map/all_gather | solution.py:66
  262.9 4.9 %fusion.23 = bf16[320,1024]{1,0:T(8,128)(2,1)} fusion(bf16[1,2048,1024]{1,2,0:T(8,128)(2,1)} %all-gather.5.cloned.1.call-done, f32[320,2048]{1,0:T(8,128)S(1)} %fusion.6), kind=kOutput, calls=%fused_computation.27 | convolution fusion | flops 1348403200 | bytes 7471104 | tf_op jit(solution)/shard_map/dot_general | solution.py:72
  267.8 7.5 %all-to-all-start.1 = ((bf16[8,40,1024]{2,1,0:T(8,128)(2,1)}), bf16[8,40,1024]{2,1,0:T(8,128)(2,1)S(1)}, u32[]{:S(2)}, u32[]{:S(2)}) async-start(bf16[8,40,1024]{2,1,0:T(8,128)(2,1)} %bitcast.4), calls=%async_computation.1 | async-start | bytes 1310720 | tf_op jit(solution)/shard_map/all_to_all | solution.py:75
  275.3 0.0 copy-done.2
  275.3 0.1 fusion.61
  275.4 0.1 div.28
  275.5 0.1 broadcast_in_dim.55
  275.6 0.0 collective-permute-done
  275.6 0.1 fusion.62
  275.7 15.6 %all-to-all-done.1 = bf16[8,40,1024]{2,1,0:T(8,128)(2,1)S(1)} async-done(((bf16[8,40,1024]{2,1,0:T(8,128)(2,1)}), bf16[8,40,1024]{2,1,0:T(8,128)(2,1)S(1)}, u32[]{:S(2)}, u32[]{:S(2)}) %all-to-all-start.1) | async-done | bytes 655392 | tf_op jit(solution)/shard_map/all_to_all | solution.py:75
  291.4 1.2 gather_fusion
  292.5 0.2 multiply_reduce_fusion
  292.8 0.1 multiply_reduce_fusion.2
  292.9 0.2 fusion.46
  293.2 0.3 fusion.57
  293.4 0.2 fusion.39
  293.7 0.4 multiply_reduce_fusion.1
  294.1 0.1 multiply_multiply_fusion.2
  294.1 0.3 fusion.50
  294.5 1.9 scatter_custom_fusion.1
  296.3 14.7 %all_to_all.20 = bf16[8,40,1024]{2,1,0:T(8,128)(2,1)S(1)} all-to-all(bf16[8,40,1024]{2,1,0:T(8,128)(2,1)S(1)} %bitcast.51), channel_id=1, replica_groups=mesh['dp'=64,'expert'=8] {'expert'}, dimensions={0} | all-to-all | bytes 1310720 | tf_op jit(solution)/shard_map/all_to_all | solution.py:126
  311.1 8.7 %fusion.20 = bf16[320,1024]{1,0:T(8,128)(2,1)} fusion(bf16[1,1024,2048]{2,1,0:T(8,128)(2,1)} %all-gather.3.cloned.1.call-done, bf16[320,1024]{1,0:T(8,128)(2,1)S(1)} %bitcast.53, bf16[1,2048,1024]{1,2,0:T(8,128)(2,1)} %all-gather.5.cloned.1.call-done, f32[320,2048]{1,0:T(8,128)} %copy-done.5), kind=kOutput, calls=%fused_computation.26 | convolution fusion | flops 2697134080 | bytes 12320768 | tf_op jit(solution)/shard_map/dot_general | solution.py:25
  319.8 3.5 all-to-all-start.3
  323.3 0.2 convolution_multiply_fusion
  323.6 12.3 %collective-permute-start.1 = (f32[4,1024]{1,0:T(4,128)S(1)}, f32[4,1024]{1,0:T(4,128)S(1)}, u32[]{:S(2)}, u32[]{:S(2)}) collective-permute-start(f32[4,1024]{1,0:T(4,128)S(1)} %convolution_multiply_fusion), channel_id=1, source_target_pairs={{8,0},{16,8},{24,16},{32,24},{40,32},{48,40},{56,48},{64,56},{72,6... | collective-permute-start | bytes 49160 | tf_op jit(solution)/shard_map/ppermute | solution.py:16
  336.0 0.3 convolution_bitcast_fusion
  336.3 101.2 %psum.7 = f32[1024,8]{0,1:T(8,128)} all-reduce(f32[1024,8]{0,1:T(8,128)S(1)} %convolution_bitcast_fusion), channel_id=1, replica_groups=mesh['dp'=64,'expert'=8] {'dp','expert'}, use_global_device_ids=true, to_apply=%region_10.11 | all-reduce | flops 8192 | bytes 65536 | tf_op jit(solution)/shard_map/psum | solution.py:124
  437.4 0.0 collective-permute-done.1
  437.4 0.4 fusion.58
  437.8 0.7 fusion.60
  438.5 0.0 all-to-all-done.3
  438.5 1.2 gather_fusion.1
  439.7 1.5 fusion.30
  (15 shorter events, 0.1 us)
Async XLA Ops:
  7.2 22.6 %copy-start = (bf16[1024,8]{0,1:T(8,128)(2,1)S(1)}, bf16[1024,8]{0,1:T(8,128)(2,1)}, u32[]{:S(2)}) copy-start(bf16[1024,8]{0,1:T(8,128)(2,1)} %param.10) | copy-start | bytes 49156
  7.2 132.4 %all-gather.3.cloned.1.call-start = ((), (), s32[]{:S(2)}) async-start(), calls=%async_computation.4 | async-start | bytes 4259840 | tf_op jit(solution)/shard_map/all_gather | solution.py:65
  7.9 255.0 %all-gather.5.cloned.1.call-start = ((), (), s32[]{:S(2)}) async-start(), calls=%async_computation.5 | async-start | bytes 4259840 | tf_op jit(solution)/shard_map/all_gather | solution.py:66
  12.5 28.9 %all-to-all-start = ((bf16[8,40,1024]{2,1,0:T(8,128)(2,1)}), bf16[8,40,1024]{2,1,0:T(8,128)(2,1)S(1)}, u32[]{:S(2)}, u32[]{:S(2)}) async-start(bf16[8,40,1024]{2,1,0:T(8,128)(2,1)} %bitcast), calls=%async_computation | async-start | bytes 1310720 | tf_op jit(solution)/shard_map/all_to_all | solution.py:54
  25.7 249.9 %collective-permute-start = (bf16[4,1024]{1,0:T(4,128)(2,1)}, bf16[4,1024]{1,0:T(4,128)(2,1)S(1)}, u32[]{:S(2)}, u32[]{:S(2)}) collective-permute-start(bf16[4,1024]{1,0:T(4,128)(2,1)} %param.13), channel_id=1, source_target_pairs={{504,0},{0,8},{8,16},{16,24},{24,32},{32,40},{40,48},{48,56},{56,6... | collective-permute-start | bytes 24584 | tf_op jit(solution)/shard_map/ppermute | solution.py:16
  143.3 124.4 %copy-start.5 = (f32[320,2048]{1,0:T(8,128)}, f32[320,2048]{1,0:T(8,128)S(1)}, u32[]{:S(2)}) copy-start(f32[320,2048]{1,0:T(8,128)S(1)} %fusion.6) | copy-start | bytes 7864324
  143.4 131.9 %copy-start.2 = (bf16[4,1024]{1,0:T(4,128)(2,1)S(1)}, bf16[4,1024]{1,0:T(4,128)(2,1)}, u32[]{:S(2)}) copy-start(bf16[4,1024]{1,0:T(4,128)(2,1)} %param.13) | copy-start | bytes 24580
  143.4 132.0 %copy-start.4 = (s32[256]{0:T(256)S(1)}, s32[256]{0:T(256)}, u32[]{:S(2)}) copy-start(s32[256]{0:T(256)} %param.9) | copy-start | bytes 3076
  267.8 23.6 %all-to-all-start.1 = ((bf16[8,40,1024]{2,1,0:T(8,128)(2,1)}), bf16[8,40,1024]{2,1,0:T(8,128)(2,1)S(1)}, u32[]{:S(2)}, u32[]{:S(2)}) async-start(bf16[8,40,1024]{2,1,0:T(8,128)(2,1)} %bitcast.4), calls=%async_computation.1 | async-start | bytes 1310720 | tf_op jit(solution)/shard_map/all_to_all | solution.py:75
  311.1 24.9 %copy-start.1 = (bf16[256,1024]{1,0:T(8,128)(2,1)S(1)}, bf16[256,1024]{1,0:T(8,128)(2,1)}, u32[]{:S(2)}) copy-start(bf16[256,1024]{1,0:T(8,128)(2,1)} %param.7) | copy-start | bytes 1572868
  311.1 24.9 %copy-start.3 = (s32[256]{0:T(256)S(1)}, s32[256]{0:T(256)}, u32[]{:S(2)}) copy-start(s32[256]{0:T(256)} %param.8) | copy-start | bytes 3076
  319.8 118.7 %all-to-all-start.3 = ((bf16[8,40,1024]{2,1,0:T(8,128)(2,1)}), bf16[8,40,1024]{2,1,0:T(8,128)(2,1)S(1)}, u32[]{:S(2)}, u32[]{:S(2)}) async-start(bf16[8,40,1024]{2,1,0:T(8,128)(2,1)} %bitcast.10), calls=%async_computation.3 | async-start | bytes 1310720 | tf_op jit(solution)/shard_map/all_to_all | solution.py:137
  323.6 113.9 %collective-permute-start.1 = (f32[4,1024]{1,0:T(4,128)S(1)}, f32[4,1024]{1,0:T(4,128)S(1)}, u32[]{:S(2)}, u32[]{:S(2)}) collective-permute-start(f32[4,1024]{1,0:T(4,128)S(1)} %convolution_multiply_fusion), channel_id=1, source_target_pairs={{8,0},{16,8},{24,16},{32,24},{40,32},{48,40},{56,48},{64,56},{72,6... | collective-permute-start | bytes 49160 | tf_op jit(solution)/shard_map/ppermute | solution.py:16
Sparse Core Ops, SparseCore 0:
  10.1 129.4 all-gather.2
  141.8 121.0 all-gather.4
where the time goes:
time: 449 us; the launch traced here: 448 us
  waiting for transfers between devices  245 us (55%)
  blocking collectives  116 us (26%)
  starting transfers between devices  40.8 us (9%)
  matrix products  22.1 us (5%)
  between operations  14.2 us (3%)
  local copies, waits for them, and re-layouts  7.48 us (2%)
    all_gather x1, waiting for transfers between devices, body(): lax.all_gather(w_out, 'dp', axis=2, tiled=True)  120 us
    psum x1, blocking collectives, body(): router_grad = lax.psum(partial_value, ('dp', 'expert'))  101 us
    all_gather x1, waiting for transfers between devices, body(): lax.all_gather(w_in, 'dp', axis=1, tiled=True)  98.3 us
    ppermute x2, starting transfers between devices, shifted(): return lax.ppermute(block, axis, route)  16.4 us
    all_to_all x1, waiting for transfers between devices, body(): lax.all_to_all(expert_out.reshape(sources, capacity, model_width), 'exper...  15.6 us
    all_to_all x1, blocking collectives, body(): lax.all_to_all(grad_buffer.reshape(experts, capacity, model_width), 'expe...  14.7 us
    all_to_all x1, starting transfers between devices, body(): lax.all_to_all(send_buffer.reshape(experts, capacity, model_width), 'expe...  13.3 us
    all_to_all x1, waiting for transfers between devices, body(): lax.all_to_all(send_buffer.reshape(experts, capacity, model_width), 'expe...  10.3 us
  transfers between devices with their start and end apart: 7, of which 4 were waited for; matrix products, arithmetic and copies ran while one was open for 4% of the time, Pallas kernels for 0%

commit v1 on v0

--- a/solution.py
+++ b/solution.py
@@ -1,3 +1,4 @@
+import functools
 import jax
 import jax.numpy as jnp
 from jax import lax
@@ -8,6 +9,14 @@
 offset = -2.0
 loss_scale = 256.0
 epsilon = 1e-06
+
+
+def record_render(load, axis_id):
+    mid_arr = lax.all_gather(load, axis_id)
+    return jnp.sum(mid_arr, axis=0)
+
+
+draw_map_all = functools.partial(record_render, axis_id=("dp", "expert"))
 
 
 def shifted(block, axis, distance):
@@ -121,7 +130,7 @@
     grad_gate = jnp.sum(grad_branch * combined, axis=1)
     grad_logits = chosen * (grad_gate * gate_values * (1.0 - gate_values) * kept_float)[:, None]
     partial_value = jnp.dot(tokens.astype(jnp.float32).T, grad_logits, precision=highest)
-    router_grad = lax.psum(partial_value, ("dp", "expert"))
+    router_grad = draw_map_all(partial_value)
     router_part = jnp.dot(grad_logits, router.astype(jnp.float32).T, precision=highest)
     grads_in = lax.all_to_all(
         grad_buffer.reshape(experts, capacity, model_width),

time: 449 us -> 1760 us (3.92)
  waiting for transfers between devices: 245 us -> 1650 us
  blocking collectives: 116 us -> 14.7 us
    all_gather x0 -> x1, waiting for transfers between devices: none -> 1400 us  [record_render(): mid_arr = lax.all_gather(load, axis_id)]
    psum x1 -> x0, blocking collectives: 101 us -> none  [body(): router_grad = lax.psum(partial_value, ('dp', 'expert'))]
  transfers between devices with their start and end apart: 7 -> 8, of which waited for: 4 -> 6; matrix products, arithmetic and copies ran while one was open for 4% -> 2% of each run, Pallas kernels for 0% -> 0%
where the time goes in v1:
time: 1760 us
  waiting for transfers between devices  1650 us (94%)
  starting transfers between devices  40.9 us (2%)
  matrix products  22.6 us (1%)
    all_gather x1, waiting for transfers between devices, record_render(): mid_arr = lax.all_gather(load, axis_id)  1400 us
    all_gather x1, waiting for transfers between devices, body(): lax.all_gather(w_out, 'dp', axis=2, tiled=True)  120 us
    all_gather x1, waiting for transfers between devices, body(): lax.all_gather(w_in, 'dp', axis=1, tiled=True)  98.2 us
  transfers between devices with their start and end apart: 8, of which 6 were waited for; matrix products, arithmetic and copies ran while one was open for 2% of the time, Pallas kernels for 0%

profile of v1, /device:TPU:1, one launch (start us, length us, event | category | flops | bytes accessed | tf_op | source)
XLA Modules:
  0.0 1759.2 jit_solution(18202166920562824703)
XLA Ops:
  7.2 0.0 copy-start
  7.2 0.0 all-gather.5.cloned.1.call-start
  7.2 0.7 all-gather.5.cloned.1.call-update
  7.9 0.0 all-gather.7.cloned.1.call-start
  8.0 0.7 all-gather.7.cloned.1.call-update
  8.7 0.7 compare_select_fusion
  9.4 3.0 scatter_custom_fusion
  12.4 13.3 all-to-all-start
  25.7 4.0 collective-permute-start
  29.7 1.3 fusion.33
  31.1 10.3 all-to-all-done
  41.3 98.2 %all-gather.5.cloned.1.call-done = bf16[1,1024,2048]{2,1,0:T(8,128)(2,1)} async-done(((bf16[1,16,2048]{2,1,0:T(8,128)(2,1)}), bf16[1,1024,2048]{2,1,0:T(8,128)(2,1)}) %all-gather.5.cloned.1.call-update) | async-done | bytes 4194320 | tf_op jit(solution)/shard_map/all_gather | solution.py:74
  139.5 3.7 fusion.6
  143.2 0.0 copy-start.2
  143.2 0.0 copy-start.4
  143.3 119.6 %all-gather.7.cloned.1.call-done = bf16[1,2048,1024]{1,2,0:T(8,128)(2,1)} async-done(((bf16[1,2048,16]{1,2,0:T(8,128)(2,1)}), bf16[1,2048,1024]{1,2,0:T(8,128)(2,1)}) %all-gather.7.cloned.1.call-update) | async-done | bytes 4194320 | tf_op jit(solution)/shard_map/all_gather | solution.py:75
  262.8 4.8 fusion.23
  267.6 7.5 all-to-all-start.1
  275.1 0.0 all-gather.9.cloned.1.call-start
  275.2 0.1 fusion.61
  275.4 0.1 div.28
  275.4 0.1 broadcast_in_dim.55
  275.5 0.1 fusion.62
  275.7 15.5 all-to-all-done.1
  291.2 1.2 gather_fusion
  292.4 0.2 multiply_reduce_fusion
  292.6 0.1 multiply_reduce_fusion.2
  292.7 0.2 fusion.46
  293.0 0.3 fusion.57
  293.3 0.2 fusion.39
  293.5 0.4 multiply_reduce_fusion.1
  293.9 0.1 multiply_multiply_fusion.2
  294.0 0.3 fusion.50
  294.3 0.9 convolution_bitcast_fusion
  295.3 0.0 all-gather.9.cloned.1.call-update
  295.3 1.9 scatter_custom_fusion.1
  297.2 14.7 all_to_all.20
  311.9 8.7 fusion.20
  320.6 3.5 all-to-all-start.3
  324.1 0.2 convolution_multiply_fusion
  324.4 12.4 collective-permute-start.1
  336.8 2.7 collective-permute-done.1
  339.5 0.4 fusion.58
  339.9 0.7 fusion.60
  340.6 1.2 gather_fusion.1
  341.7 1.5 fusion.30
  343.2 1402.1 %all-gather.9.cloned.1.call-done = f32[524288,8]{0,1:T(8,128)} async-done(((f32[1024,8]{0,1:T(8,128)}), f32[524288,8]{0,1:T(8,128)}) %all-gather.9.cloned.1.call-update) | async-done | bytes 16777232 | tf_op jit(solution)/shard_map/all_gather | solution.py:15
  1745.3 7.4 reduce_sum.89
  (18 shorter events, 0.1 us)
Async XLA Ops:
  7.2 22.6 %copy-start = (bf16[1024,8]{0,1:T(8,128)(2,1)S(1)}, bf16[1024,8]{0,1:T(8,128)(2,1)}, u32[]{:S(2)}) copy-start(bf16[1024,8]{0,1:T(8,128)(2,1)} %param.10) | copy-start | bytes 49156
  7.2 132.3 %all-gather.5.cloned.1.call-start = ((), (), s32[]{:S(2)}) async-start(), calls=%async_computation.4 | async-start | bytes 4259840 | tf_op jit(solution)/shard_map/all_gather | solution.py:74
  7.9 254.9 %all-gather.7.cloned.1.call-start = ((), (), s32[]{:S(2)}) async-start(), calls=%async_computation.5 | async-start | bytes 4259840 | tf_op jit(solution)/shard_map/all_gather | solution.py:75
  12.4 28.9 %all-to-all-start = ((bf16[8,40,1024]{2,1,0:T(8,128)(2,1)}), bf16[8,40,1024]{2,1,0:T(8,128)(2,1)S(1)}, u32[]{:S(2)}, u32[]{:S(2)}) async-start(bf16[8,40,1024]{2,1,0:T(8,128)(2,1)} %bitcast), calls=%async_computation | async-start | bytes 1310720 | tf_op jit(solution)/shard_map/all_to_all | solution.py:63
  25.7 249.8 %collective-permute-start = (bf16[4,1024]{1,0:T(4,128)(2,1)}, bf16[4,1024]{1,0:T(4,128)(2,1)S(1)}, u32[]{:S(2)}, u32[]{:S(2)}) collective-permute-start(bf16[4,1024]{1,0:T(4,128)(2,1)} %param.13), channel_id=1, source_target_pairs={{504,0},{0,8},{8,16},{16,24},{24,32},{32,40},{40,48},{48,56},{56,6... | collective-permute-start | bytes 24584 | tf_op jit(solution)/shard_map/ppermute | solution.py:25
  143.2 124.4 %copy-start.5 = (f32[320,2048]{1,0:T(8,128)}, f32[320,2048]{1,0:T(8,128)S(1)}, u32[]{:S(2)}) copy-start(f32[320,2048]{1,0:T(8,128)S(1)} %fusion.6) | copy-start | bytes 7864324
  143.2 131.9 %copy-start.2 = (bf16[4,1024]{1,0:T(4,128)(2,1)S(1)}, bf16[4,1024]{1,0:T(4,128)(2,1)}, u32[]{:S(2)}) copy-start(bf16[4,1024]{1,0:T(4,128)(2,1)} %param.13) | copy-start | bytes 24580
  143.2 132.1 %copy-start.4 = (s32[256]{0:T(256)S(1)}, s32[256]{0:T(256)}, u32[]{:S(2)}) copy-start(s32[256]{0:T(256)} %param.9) | copy-start | bytes 3076
  267.6 23.6 %all-to-all-start.1 = ((bf16[8,40,1024]{2,1,0:T(8,128)(2,1)}), bf16[8,40,1024]{2,1,0:T(8,128)(2,1)S(1)}, u32[]{:S(2)}, u32[]{:S(2)}) async-start(bf16[8,40,1024]{2,1,0:T(8,128)(2,1)} %bitcast.4), calls=%async_computation.1 | async-start | bytes 1310720 | tf_op jit(solution)/shard_map/all_to_all | solution.py:84
  275.1 1470.2 %all-gather.9.cloned.1.call-start = ((), (), s32[]{:S(2)}) async-start(), calls=%async_computation.6 | async-start | bytes 16809984 | tf_op jit(solution)/shard_map/all_gather | solution.py:15
  291.2 3.1 copy-start.1
  291.2 3.1 copy-start.3
  320.6 20.0 %all-to-all-start.3 = ((bf16[8,40,1024]{2,1,0:T(8,128)(2,1)}), bf16[8,40,1024]{2,1,0:T(8,128)(2,1)S(1)}, u32[]{:S(2)}, u32[]{:S(2)}) async-start(bf16[8,40,1024]{2,1,0:T(8,128)(2,1)} %bitcast.10), calls=%async_computation.3 | async-start | bytes 1310720 | tf_op jit(solution)/shard_map/all_to_all | solution.py:146
  324.4 15.1 collective-permute-start.1
Sparse Core Ops, SparseCore 0:
  10.1 129.3 all-gather.4
  141.7 121.1 all-gather.6
  295.4 1449.8 all-gather.8
